TPU v7x, 32 devices: a whole 2x2x4 slice. The times are simulated.
32 devices in a mesh: ab: 16 (over z, y, core), ij: 2 (over x).
Axes of the slice: x: 2, y: 2, z: 4, core: 2. Of those that a mesh axis runs over, the one named last changes fastest.
Arguments:
- amplitudes: float32 [128, 2048], P('ab', 'ij'), may hold values from -6 to 6
- integrals: float32 [16384, 2048], P('ab'), may hold values from -0.125 to 0.125
- occ_pairs: float32 [128], P(('ab', 'ij')), may hold values from -2 to -0.5
- vir_pairs: float32 [16384], P('ab'), may hold values from 1 to 4
Outputs:
- update: float32 [128, 16384], P(('ab', 'ij'))
All inputs are finite; a program needn't handle non-finite values.
Results may differ from a plain program's by a relative error of at most 0.00007.
Values sent between devices are 32-bit elements; how exact they have to be, the bound alone decides.
No kernel may reach another device: no remote copies, remote signals or barrier semaphores. Data moves between devices by JAX's collectives and lax.ppermute only.
A program may use at most 64 MiB of HBM per device.

v0:
```python
import jax
import jax.numpy as jnp
from jax import lax
from jax.sharding import PartitionSpec as P


def contract(block_amps, integrals):
    return lax.dot_general(
        block_amps,
        integrals,
        (((1,), (1,)), ((), ())),
        precision=lax.Precision.HIGHEST,
        preferred_element_type=jnp.float32,
    )


def shards(amplitudes, integrals, occ_pairs, vir_pairs):
    arrived = lax.all_to_all(amplitudes, "ij", split_axis=0, concat_axis=1, tiled=True)
    slice_amps = lax.all_gather(arrived, "ab", axis=0, tiled=True)
    row_energy = lax.all_gather(occ_pairs, "ab", axis=0, tiled=True)
    groups = lax.axis_size("ab")
    per_device = occ_pairs.shape[0]
    panel_cols = integrals.shape[1]
    grouped = slice_amps.reshape(groups, per_device, panel_cols)
    energy_grouped = row_energy.reshape(groups, per_device)
    block_amps = grouped.reshape(-1, panel_cols)
    residual = contract(block_amps, integrals)
    block_energy = energy_grouped.reshape(-1)
    residual = residual / (vir_pairs[None, :] - block_energy[:, None])
    moved = lax.all_to_all(residual, "ab", split_axis=0, concat_axis=1, tiled=True)
    return moved


def solution(mesh):
    return jax.shard_map(
        shards,
        mesh=mesh,
        in_specs=(P("ab", "ij"), P("ab", None), P(("ab", "ij")), P("ab")),
        out_specs=P(("ab", "ij"), None),
        check_vma=False,
    )
```

profile of v0, /device:TPU:0, one launch (start us, length us, event | category | flops | bytes accessed | tf_op | source)
XLA Modules:
  0.0 86.3 jit_solution(3729236758331604290)
XLA Ops:
  0.0 1.4 %all_to_all.28 = f32[2,4,1024]{2,1,0:T(4,128)} reshape(f32[8,1024]{1,0:T(8,128)} %param.4) | data formatting | bytes 65536 | tf_op jit(solution)/shard_map/all_to_all | solution.py:18
  1.4 4.2 %all-to-all-start = ((f32[2,4,1024]{2,1,0:T(4,128)}), f32[2,4,1024]{2,1,0:T(4,128)S(1)}, u32[]{:S(2)}, u32[]{:S(2)}) async-start(f32[2,4,1024]{2,1,0:T(4,128)} %all_to_all.28), calls=%async_computation | async-start | bytes 65536 | tf_op jit(solution)/shard_map/all_to_all | solution.py:18
  5.6 1.3 %dynamic-slice = u32[1]{0:T(128)} dynamic-slice(u32[32]{0:T(128)} %constant.4, u32[]{:T(128)S(6)} %add), dynamic_slice_sizes={1} | dynamic-slice | bytes 12
  7.6 0.9 dynamic-update-slice
  8.5 34.0 %all-reduce = f32[64]{0:T(128)S(1)} all-reduce(f32[64]{0:T(128)S(1)} %dynamic-update-slice), channel_id=1, replica_groups=mesh['ab'=16,'ij'=2] {'ab'}, use_global_device_ids=true, to_apply=%add | all-reduce | flops 64 | bytes 512
  42.5 0.0 all-to-all-done
  42.5 18.7 %all-gather = f32[16,4,2048]{2,1,0:T(4,128)S(1)} all-gather(f32[1,4,2048]{2,1,0:T(4,128)S(1)} %bitcast.10), channel_id=1, replica_groups=mesh['ab'=16,'ij'=2] {'ab'}, dimensions={0}, use_global_device_ids=true | all-gather | bytes 557056 | tf_op jit(solution)/shard_map/all_gather | solution.py:19
  61.2 0.2 reshape.12
  61.4 10.5 %convolution_divide_fusion = f32[64,1024]{1,0:T(8,128)S(1)} fusion(f32[64,2048]{1,0:T(8,128)S(1)} %reshape.12, f32[1024,2048]{1,0:T(8,128)} %param.5, f32[64]{0:T(128)S(1)} %all-reduce, f32[1024]{0:T(1024)} %param.7), kind=kOutput, calls=%fused_computation | convolution fusion | flops 1610743808 | bytes 9179392 | tf_op jit(solution)/shard_map/dot_general | solution.py:8
  71.9 0.1 all_to_all.32
  72.0 13.6 %all_to_all.38 = f32[16,4,1024]{2,1,0:T(4,128)S(1)} all-to-all(f32[16,4,1024]{2,1,0:T(4,128)S(1)} %all_to_all.32), channel_id=1, replica_groups=mesh['ab'=16,'ij'=2] {'ab'}, dimensions={0} | all-to-all | bytes 524288 | tf_op jit(solution)/shard_map/all_to_all | solution.py:30
  85.6 0.7 copy.11
  (1 shorter events, 0.0 us)
Async XLA Ops:
  1.4 41.1 %all-to-all-start = ((f32[2,4,1024]{2,1,0:T(4,128)}), f32[2,4,1024]{2,1,0:T(4,128)S(1)}, u32[]{:S(2)}, u32[]{:S(2)}) async-start(f32[2,4,1024]{2,1,0:T(4,128)} %all_to_all.28), calls=%async_computation | async-start | bytes 65536 | tf_op jit(solution)/shard_map/all_to_all | solution.py:18
where the time goes:
time: 86.6 us; the launch traced here: 86.3 us
  blocking collectives  66.3 us (77%)
  matrix products  10.5 us (12%)
  local copies, waits for them, and re-layouts  4.52 us (5%)
  starting transfers between devices  4.23 us (5%)
    unnamed x1, blocking collectives  34 us
    all_gather x1, blocking collectives, shards(): slice_amps = lax.all_gather(arrived, 'ab', axis=0, tiled=True)  18.7 us
    all_to_all x1, blocking collectives, shards(): lax.all_to_all(residual, 'ab', split_axis=0, concat_axis=1, tiled=True)  13.6 us
    dot_general x1, matrix products, contract(): lax.dot_general(block_amps, integrals, (((1,), (1,)), ((), ())), precisio...  10.5 us
    all_to_all x1, starting transfers between devices, shards(): lax.all_to_all(amplitudes, 'ij', split_axis=0, concat_axis=1, tiled=True)  4.23 us
    unnamed x5, local copies, waits for them, and re-layouts  3.06 us
  transfers between devices with their start and end apart: 1, of which 0 were waited for; matrix products, arithmetic and copies ran while one was open for 3% of the time, Pallas kernels for 0%

commit v1 on v0

--- a/solution.py
+++ b/solution.py
@@ -16,7 +16,12 @@
 
 def shards(amplitudes, integrals, occ_pairs, vir_pairs):
     arrived = lax.all_to_all(amplitudes, "ij", split_axis=0, concat_axis=1, tiled=True)
-    slice_amps = lax.all_gather(arrived, "ab", axis=0, tiled=True)
+    ring = [arrived]
+    for hop in range(15):
+        ring.append(lax.ppermute(ring[-1], "ab", [(dev, (dev + 1) % 16) for dev in range(16)]))
+    slice_amps = jnp.roll(
+        jnp.concatenate(ring[::-1], axis=0), (lax.axis_index("ab") + 1) * ring[0].shape[0], axis=0
+    )
     row_energy = lax.all_gather(occ_pairs, "ab", axis=0, tiled=True)
     groups = lax.axis_size("ab")
     per_device = occ_pairs.shape[0]

time: 86.6 us -> 155 us (1.79)
  waiting for transfers between devices: 0.01 us -> 84.5 us
  blocking collectives: 66.3 us -> 54.5 us
  starting transfers between devices: 4.23 us -> 0.04 us
    ppermute x0 -> x15, waiting for transfers between devices: none -> 84.5 us  [shards(): lax.ppermute(ring[-1], 'ab', [(dev, (dev + 1) % 16) for dev in range(16)])]
    all_gather x1 -> x0, blocking collectives: 18.7 us -> none  [shards(): slice_amps = lax.all_gather(arrived, 'ab', axis=0, tiled=True)]
    all_to_all x0 -> x1, blocking collectives: none -> 7.98 us  [shards(): lax.all_to_all(amplitudes, 'ij', split_axis=0, concat_axis=1, tiled=True)]
    all_to_all x1 -> x0, starting transfers between devices: 4.23 us -> none  [shards(): lax.all_to_all(amplitudes, 'ij', split_axis=0, concat_axis=1, tiled=True)]
  transfers between devices with their start and end apart: 1 -> 15, of which waited for: 0 -> 14; matrix products, arithmetic and copies ran while one was open for 3% -> 1% of each run, Pallas kernels for 0% -> 0%
where the time goes in v1:
time: 155 us; the launch traced here: 154 us
  waiting for transfers between devices  84.5 us (55%)
  blocking collectives  54.5 us (35%)
  matrix products  10.5 us (7%)
  local copies, waits for them, and re-layouts  4.24 us (3%)
    ppermute x15, waiting for transfers between devices, shards(): lax.ppermute(ring[-1], 'ab', [(dev, (dev + 1) % 16) for dev in range(16)])  84.5 us
    unnamed x1, blocking collectives  33.9 us
    all_to_all x1, blocking collectives, shards(): lax.all_to_all(residual, 'ab', split_axis=0, concat_axis=1, tiled=True)  12.6 us
    dot_general x1, matrix products, contract(): lax.dot_general(block_amps, integrals, (((1,), (1,)), ((), ())), precisio...  10.5 us
    all_to_all x1, blocking collectives, shards(): lax.all_to_all(amplitudes, 'ij', split_axis=0, concat_axis=1, tiled=True)  7.98 us
  transfers between devices with their start and end apart: 15, of which 14 were waited for; matrix products, arithmetic and copies ran while one was open for 1% of the time, Pallas kernels for 0%

profile of v1, /device:TPU:0, one launch (start us, length us, event | category | flops | bytes accessed | tf_op | source)
XLA Modules:
  0.0 154.5 jit_solution(9190398517280148582)
XLA Ops:
  0.0 0.8 all_to_all.28
  0.8 8.0 %all_to_all.38 = f32[2,4,1024]{2,1,0:T(4,128)S(1)} all-to-all(f32[2,4,1024]{2,1,0:T(4,128)S(1)} %all_to_all.28), channel_id=1, replica_groups=mesh['ab'=16,'ij'=2] {'ij'}, dimensions={0} | all-to-all | bytes 65536 | tf_op jit(solution)/shard_map/all_to_all | solution.py:18
  8.8 0.0 collective-permute-start
  8.8 6.0 %collective-permute-done = f32[4,2048]{1,0:T(4,128)S(1)} collective-permute-done((f32[4,2048]{1,0:T(4,128)S(1)}, f32[4,2048]{1,0:T(4,128)S(1)}, u32[]{:S(2)}, u32[]{:S(2)}) %collective-permute-start) | collective-permute-done | bytes 32800 | tf_op jit(solution)/shard_map/ppermute | solution.py:21
  14.8 0.0 collective-permute-start.1
  14.8 6.0 %collective-permute-done.1 = f32[4,2048]{1,0:T(4,128)S(1)} collective-permute-done((f32[4,2048]{1,0:T(4,128)S(1)}, f32[4,2048]{1,0:T(4,128)S(1)}, u32[]{:S(2)}, u32[]{:S(2)}) %collective-permute-start.1) | collective-permute-done | bytes 32800 | tf_op jit(solution)/shard_map/ppermute | solution.py:21
  20.8 0.0 collective-permute-start.2
  20.8 6.0 %collective-permute-done.2 = f32[4,2048]{1,0:T(4,128)S(1)} collective-permute-done((f32[4,2048]{1,0:T(4,128)S(1)}, f32[4,2048]{1,0:T(4,128)S(1)}, u32[]{:S(2)}, u32[]{:S(2)}) %collective-permute-start.2) | collective-permute-done | bytes 32800 | tf_op jit(solution)/shard_map/ppermute | solution.py:21
  26.9 0.0 collective-permute-start.3
  26.9 6.0 %collective-permute-done.3 = f32[4,2048]{1,0:T(4,128)S(1)} collective-permute-done((f32[4,2048]{1,0:T(4,128)S(1)}, f32[4,2048]{1,0:T(4,128)S(1)}, u32[]{:S(2)}, u32[]{:S(2)}) %collective-permute-start.3) | collective-permute-done | bytes 32800 | tf_op jit(solution)/shard_map/ppermute | solution.py:21
  32.9 0.0 collective-permute-start.4
  32.9 6.0 %collective-permute-done.4 = f32[4,2048]{1,0:T(4,128)S(1)} collective-permute-done((f32[4,2048]{1,0:T(4,128)S(1)}, f32[4,2048]{1,0:T(4,128)S(1)}, u32[]{:S(2)}, u32[]{:S(2)}) %collective-permute-start.4) | collective-permute-done | bytes 32800 | tf_op jit(solution)/shard_map/ppermute | solution.py:21
  38.9 0.0 collective-permute-start.5
  38.9 6.0 %collective-permute-done.5 = f32[4,2048]{1,0:T(4,128)S(1)} collective-permute-done((f32[4,2048]{1,0:T(4,128)S(1)}, f32[4,2048]{1,0:T(4,128)S(1)}, u32[]{:S(2)}, u32[]{:S(2)}) %collective-permute-start.5) | collective-permute-done | bytes 32800 | tf_op jit(solution)/shard_map/ppermute | solution.py:21
  45.0 0.0 collective-permute-start.6
  45.0 6.0 %collective-permute-done.6 = f32[4,2048]{1,0:T(4,128)S(1)} collective-permute-done((f32[4,2048]{1,0:T(4,128)S(1)}, f32[4,2048]{1,0:T(4,128)S(1)}, u32[]{:S(2)}, u32[]{:S(2)}) %collective-permute-start.6) | collective-permute-done | bytes 32800 | tf_op jit(solution)/shard_map/ppermute | solution.py:21
  51.0 0.0 collective-permute-start.7
  51.0 6.0 %collective-permute-done.7 = f32[4,2048]{1,0:T(4,128)S(1)} collective-permute-done((f32[4,2048]{1,0:T(4,128)S(1)}, f32[4,2048]{1,0:T(4,128)S(1)}, u32[]{:S(2)}, u32[]{:S(2)}) %collective-permute-start.7) | collective-permute-done | bytes 32800 | tf_op jit(solution)/shard_map/ppermute | solution.py:21
  57.1 0.0 collective-permute-start.8
  57.1 6.0 %collective-permute-done.8 = f32[4,2048]{1,0:T(4,128)S(1)} collective-permute-done((f32[4,2048]{1,0:T(4,128)S(1)}, f32[4,2048]{1,0:T(4,128)S(1)}, u32[]{:S(2)}, u32[]{:S(2)}) %collective-permute-start.8) | collective-permute-done | bytes 32800 | tf_op jit(solution)/shard_map/ppermute | solution.py:21
  63.1 0.0 collective-permute-start.9
  63.1 6.0 %collective-permute-done.9 = f32[4,2048]{1,0:T(4,128)S(1)} collective-permute-done((f32[4,2048]{1,0:T(4,128)S(1)}, f32[4,2048]{1,0:T(4,128)S(1)}, u32[]{:S(2)}, u32[]{:S(2)}) %collective-permute-start.9) | collective-permute-done | bytes 32800 | tf_op jit(solution)/shard_map/ppermute | solution.py:21
  69.1 0.0 collective-permute-start.10
  69.1 6.0 %collective-permute-done.10 = f32[4,2048]{1,0:T(4,128)S(1)} collective-permute-done((f32[4,2048]{1,0:T(4,128)S(1)}, f32[4,2048]{1,0:T(4,128)S(1)}, u32[]{:S(2)}, u32[]{:S(2)}) %collective-permute-start.10) | collective-permute-done | bytes 32800 | tf_op jit(solution)/shard_map/ppermute | solution.py:21
  75.2 0.0 collective-permute-start.11
  75.2 6.0 %collective-permute-done.11 = f32[4,2048]{1,0:T(4,128)S(1)} collective-permute-done((f32[4,2048]{1,0:T(4,128)S(1)}, f32[4,2048]{1,0:T(4,128)S(1)}, u32[]{:S(2)}, u32[]{:S(2)}) %collective-permute-start.11) | collective-permute-done | bytes 32800 | tf_op jit(solution)/shard_map/ppermute | solution.py:21
  81.2 0.0 collective-permute-start.12
  81.2 6.0 %collective-permute-done.12 = f32[4,2048]{1,0:T(4,128)S(1)} collective-permute-done((f32[4,2048]{1,0:T(4,128)S(1)}, f32[4,2048]{1,0:T(4,128)S(1)}, u32[]{:S(2)}, u32[]{:S(2)}) %collective-permute-start.12) | collective-permute-done | bytes 32800 | tf_op jit(solution)/shard_map/ppermute | solution.py:21
  87.2 0.0 collective-permute-start.13
  87.2 6.0 %collective-permute-done.13 = f32[4,2048]{1,0:T(4,128)S(1)} collective-permute-done((f32[4,2048]{1,0:T(4,128)S(1)}, f32[4,2048]{1,0:T(4,128)S(1)}, u32[]{:S(2)}, u32[]{:S(2)}) %collective-permute-start.13) | collective-permute-done | bytes 32800 | tf_op jit(solution)/shard_map/ppermute | solution.py:21
  93.3 0.0 collective-permute-start.14
  93.3 1.2 dynamic-slice
  95.2 0.9 dynamic-update-slice
  96.0 33.9 %all-reduce = f32[64]{0:T(128)S(1)} all-reduce(f32[64]{0:T(128)S(1)} %dynamic-update-slice), channel_id=1, replica_groups=mesh['ab'=16,'ij'=2] {'ab'}, use_global_device_ids=true, to_apply=%add | all-reduce | flops 64 | bytes 512
  129.9 0.0 collective-permute-done.14
  129.9 0.6 concatenate.6
  130.5 10.5 %convolution_divide_fusion = f32[64,1024]{1,0:T(8,128)S(1)} fusion(f32[1024,2048]{1,0:T(8,128)} %param.5, f32[128,2048]{1,0:T(8,128)S(1)} %concatenate.6, s32[]{:T(128)S(6)} %select_n.14, f32[64]{0:T(128)S(1)} %all-reduce, f32[1024]{0:T(1024)} %param.7), kind=kOutput, calls=%fused_computation | convolution fusion | flops 1610743808 | bytes 9179652 | tf_op jit(solution)/shard_map/dot_general | solution.py:8
  141.1 0.1 all_to_all.32
  141.1 12.6 %all_to_all.39 = f32[16,4,1024]{2,1,0:T(4,128)S(1)} all-to-all(f32[16,4,1024]{2,1,0:T(4,128)S(1)} %all_to_all.32), channel_id=1, replica_groups=mesh['ab'=16,'ij'=2] {'ab'}, dimensions={0} | all-to-all | bytes 524288 | tf_op jit(solution)/shard_map/all_to_all | solution.py:35
  153.7 0.7 copy.8
  (1 shorter events, 0.0 us)
Async XLA Ops:
  8.8 6.0 %collective-permute-start = (f32[4,2048]{1,0:T(4,128)S(1)}, f32[4,2048]{1,0:T(4,128)S(1)}, u32[]{:S(2)}, u32[]{:S(2)}) collective-permute-start(f32[4,2048]{1,0:T(4,128)S(1)} %bitcast.9), channel_id=1, source_target_pairs={{0,2},{2,4},{4,6},{6,8},{8,10},{10,12},{12,14},{14,16},{16,18},{18... | collective-permute-start | bytes 98312 | tf_op jit(solution)/shard_map/ppermute | solution.py:21
  14.8 6.0 %collective-permute-start.1 = (f32[4,2048]{1,0:T(4,128)S(1)}, f32[4,2048]{1,0:T(4,128)S(1)}, u32[]{:S(2)}, u32[]{:S(2)}) collective-permute-start(f32[4,2048]{1,0:T(4,128)S(1)} %collective-permute-done), channel_id=1, source_target_pairs={{0,2},{2,4},{4,6},{6,8},{8,10},{10,12},{12,14},{14,16},{16,18},{18... | collective-permute-start | bytes 98312 | tf_op jit(solution)/shard_map/ppermute | solution.py:21
  20.8 6.0 %collective-permute-start.2 = (f32[4,2048]{1,0:T(4,128)S(1)}, f32[4,2048]{1,0:T(4,128)S(1)}, u32[]{:S(2)}, u32[]{:S(2)}) collective-permute-start(f32[4,2048]{1,0:T(4,128)S(1)} %collective-permute-done.1), channel_id=1, source_target_pairs={{0,2},{2,4},{4,6},{6,8},{8,10},{10,12},{12,14},{14,16},{16,18},{18... | collective-permute-start | bytes 98312 | tf_op jit(solution)/shard_map/ppermute | solution.py:21
  26.9 6.0 %collective-permute-start.3 = (f32[4,2048]{1,0:T(4,128)S(1)}, f32[4,2048]{1,0:T(4,128)S(1)}, u32[]{:S(2)}, u32[]{:S(2)}) collective-permute-start(f32[4,2048]{1,0:T(4,128)S(1)} %collective-permute-done.2), channel_id=1, source_target_pairs={{0,2},{2,4},{4,6},{6,8},{8,10},{10,12},{12,14},{14,16},{16,18},{18... | collective-permute-start | bytes 98312 | tf_op jit(solution)/shard_map/ppermute | solution.py:21
  32.9 6.0 %collective-permute-start.4 = (f32[4,2048]{1,0:T(4,128)S(1)}, f32[4,2048]{1,0:T(4,128)S(1)}, u32[]{:S(2)}, u32[]{:S(2)}) collective-permute-start(f32[4,2048]{1,0:T(4,128)S(1)} %collective-permute-done.3), channel_id=1, source_target_pairs={{0,2},{2,4},{4,6},{6,8},{8,10},{10,12},{12,14},{14,16},{16,18},{18... | collective-permute-start | bytes 98312 | tf_op jit(solution)/shard_map/ppermute | solution.py:21
  38.9 6.0 %collective-permute-start.5 = (f32[4,2048]{1,0:T(4,128)S(1)}, f32[4,2048]{1,0:T(4,128)S(1)}, u32[]{:S(2)}, u32[]{:S(2)}) collective-permute-start(f32[4,2048]{1,0:T(4,128)S(1)} %collective-permute-done.4), channel_id=1, source_target_pairs={{0,2},{2,4},{4,6},{6,8},{8,10},{10,12},{12,14},{14,16},{16,18},{18... | collective-permute-start | bytes 98312 | tf_op jit(solution)/shard_map/ppermute | solution.py:21
  45.0 6.0 %collective-permute-start.6 = (f32[4,2048]{1,0:T(4,128)S(1)}, f32[4,2048]{1,0:T(4,128)S(1)}, u32[]{:S(2)}, u32[]{:S(2)}) collective-permute-start(f32[4,2048]{1,0:T(4,128)S(1)} %collective-permute-done.5), channel_id=1, source_target_pairs={{0,2},{2,4},{4,6},{6,8},{8,10},{10,12},{12,14},{14,16},{16,18},{18... | collective-permute-start | bytes 98312 | tf_op jit(solution)/shard_map/ppermute | solution.py:21
  51.0 6.0 %collective-permute-start.7 = (f32[4,2048]{1,0:T(4,128)S(1)}, f32[4,2048]{1,0:T(4,128)S(1)}, u32[]{:S(2)}, u32[]{:S(2)}) collective-permute-start(f32[4,2048]{1,0:T(4,128)S(1)} %collective-permute-done.6), channel_id=1, source_target_pairs={{0,2},{2,4},{4,6},{6,8},{8,10},{10,12},{12,14},{14,16},{16,18},{18... | collective-permute-start | bytes 98312 | tf_op jit(solution)/shard_map/ppermute | solution.py:21
  57.1 6.0 %collective-permute-start.8 = (f32[4,2048]{1,0:T(4,128)S(1)}, f32[4,2048]{1,0:T(4,128)S(1)}, u32[]{:S(2)}, u32[]{:S(2)}) collective-permute-start(f32[4,2048]{1,0:T(4,128)S(1)} %collective-permute-done.7), channel_id=1, source_target_pairs={{0,2},{2,4},{4,6},{6,8},{8,10},{10,12},{12,14},{14,16},{16,18},{18... | collective-permute-start | bytes 98312 | tf_op jit(solution)/shard_map/ppermute | solution.py:21
  63.1 6.0 %collective-permute-start.9 = (f32[4,2048]{1,0:T(4,128)S(1)}, f32[4,2048]{1,0:T(4,128)S(1)}, u32[]{:S(2)}, u32[]{:S(2)}) collective-permute-start(f32[4,2048]{1,0:T(4,128)S(1)} %collective-permute-done.8), channel_id=1, source_target_pairs={{0,2},{2,4},{4,6},{6,8},{8,10},{10,12},{12,14},{14,16},{16,18},{18... | collective-permute-start | bytes 98312 | tf_op jit(solution)/shard_map/ppermute | solution.py:21
  69.1 6.0 %collective-permute-start.10 = (f32[4,2048]{1,0:T(4,128)S(1)}, f32[4,2048]{1,0:T(4,128)S(1)}, u32[]{:S(2)}, u32[]{:S(2)}) collective-permute-start(f32[4,2048]{1,0:T(4,128)S(1)} %collective-permute-done.9), channel_id=1, source_target_pairs={{0,2},{2,4},{4,6},{6,8},{8,10},{10,12},{12,14},{14,16},{16,18},{18... | collective-permute-start | bytes 98312 | tf_op jit(solution)/shard_map/ppermute | solution.py:21
  75.2 6.0 %collective-permute-start.11 = (f32[4,2048]{1,0:T(4,128)S(1)}, f32[4,2048]{1,0:T(4,128)S(1)}, u32[]{:S(2)}, u32[]{:S(2)}) collective-permute-start(f32[4,2048]{1,0:T(4,128)S(1)} %collective-permute-done.10), channel_id=1, source_target_pairs={{0,2},{2,4},{4,6},{6,8},{8,10},{10,12},{12,14},{14,16},{16,18},{18... | collective-permute-start | bytes 98312 | tf_op jit(solution)/shard_map/ppermute | solution.py:21
  81.2 6.0 %collective-permute-start.12 = (f32[4,2048]{1,0:T(4,128)S(1)}, f32[4,2048]{1,0:T(4,128)S(1)}, u32[]{:S(2)}, u32[]{:S(2)}) collective-permute-start(f32[4,2048]{1,0:T(4,128)S(1)} %collective-permute-done.11), channel_id=1, source_target_pairs={{0,2},{2,4},{4,6},{6,8},{8,10},{10,12},{12,14},{14,16},{16,18},{18... | collective-permute-start | bytes 98312 | tf_op jit(solution)/shard_map/ppermute | solution.py:21
  87.2 6.0 %collective-permute-start.13 = (f32[4,2048]{1,0:T(4,128)S(1)}, f32[4,2048]{1,0:T(4,128)S(1)}, u32[]{:S(2)}, u32[]{:S(2)}) collective-permute-start(f32[4,2048]{1,0:T(4,128)S(1)} %collective-permute-done.12), channel_id=1, source_target_pairs={{0,2},{2,4},{4,6},{6,8},{8,10},{10,12},{12,14},{14,16},{16,18},{18... | collective-permute-start | bytes 98312 | tf_op jit(solution)/shard_map/ppermute | solution.py:21
  93.3 36.7 %collective-permute-start.14 = (f32[4,2048]{1,0:T(4,128)S(1)}, f32[4,2048]{1,0:T(4,128)S(1)}, u32[]{:S(2)}, u32[]{:S(2)}) collective-permute-start(f32[4,2048]{1,0:T(4,128)S(1)} %collective-permute-done.13), channel_id=1, source_target_pairs={{0,2},{2,4},{4,6},{6,8},{8,10},{10,12},{12,14},{14,16},{16,18},{18... | collective-permute-start | bytes 98312 | tf_op jit(solution)/shard_map/ppermute | solution.py:21
